TPU v7x, 256 devices: a whole 4x4x8 slice. The times are simulated.
256 devices in a mesh: dp: 2 (over core), ctx: 32 (over y, z), grp: 4 (over x).
Axes of the slice: x: 4, y: 4, z: 8, core: 2. Of those that a mesh axis runs over, the one named last changes fastest.
Arguments:
- projected: bfloat16 [4, 8192, 3, 4096], P('dp', 'ctx', None, 'grp'), may hold values from -6 to 6
- short_w: float32 [3, 3, 4096], P(None, None, 'grp'), may hold values from -2.5 to 2.5
- medium_h: bfloat16 [256, 128], P('grp'), may hold values from -3 to 3
- out_w: bfloat16 [4096, 4096], P('ctx', 'grp'), may hold values from -0.09375 to 0.09375
- grad_out: bfloat16 [4, 8192, 4096], P('dp', 'ctx', 'grp'), may hold values from -6 to 6
Outputs:
- block_out: bfloat16 [4, 8192, 4096], P('dp', 'ctx', 'grp')
- grad_projected: bfloat16 [4, 8192, 3, 4096], P('dp', 'ctx', None, 'grp')
- filter_grad: float32 [256, 128], P('grp')
- short_grad: float32 [3, 3, 4096], P(None, None, 'grp')
All inputs are finite; a program needn't handle non-finite values.
Results may differ from a plain program's by a relative error of at most 0.0064.
Values may be sent and summed in bfloat16 or wider, within the bound.
A program may use at most 128 MiB of HBM per device.

v0:
```python
import math
import jax
import jax.numpy as jnp
from jax import lax
from jax.sharding import PartitionSpec as P


def from_behind(block, axis, distance):
    devices = range(lax.axis_size(axis))
    route = [(i - distance, i) for i in devices if i - distance in devices]
    return lax.ppermute(block, axis, route)


def windows(padded, block_rows, reach):
    seqs_here = padded.shape[0]
    block_count = (padded.shape[1] - reach) // block_rows
    extended = jnp.pad(padded, ((0, 0), (0, block_rows - reach), (0, 0), (0, 0)))
    leading = extended[:, : block_count * block_rows].reshape(
        seqs_here, block_count, block_rows, padded.shape[2], padded.shape[3]
    )
    second = extended[:, block_rows:].reshape(
        seqs_here, block_count, block_rows, padded.shape[2], padded.shape[3]
    )[:, :, :reach]
    return jnp.concatenate([leading, second], axis=2)


def banded(filters, block_rows):
    groups_here = filters.shape[0]
    tap_count = filters.shape[1]
    line_width = block_rows + tap_count
    padded_line = jnp.concatenate(
        [filters, jnp.zeros((groups_here, block_rows), filters.dtype)], axis=1
    )
    tiled = jnp.broadcast_to(
        padded_line[:, None, :], (groups_here, block_rows, line_width)
    ).reshape(groups_here, block_rows * line_width)
    return tiled[:, : block_rows * (line_width - 1)].reshape(
        groups_here, block_rows, line_width - 1
    )


def band_conv(turned, matrix, block_rows):
    reach = matrix.shape[2] - block_rows
    windowed = windows(turned, block_rows, reach)
    result = jnp.einsum("gtj,sbjcg->sbtcg", matrix, windowed, preferred_element_type=jnp.float32)
    result = jnp.swapaxes(result, 3, 4)
    return result.reshape(
        turned.shape[0], turned.shape[1] - reach, turned.shape[2] * turned.shape[3]
    )


def lag_sums(grad_blocks, windowed, tap_count):
    products = jnp.einsum(
        "sbtcg,sbjcg->gtj", grad_blocks, windowed, preferred_element_type=jnp.float32
    )
    groups_here = products.shape[0]
    block_rows = products.shape[1]
    line_width = products.shape[2]
    flat_rows = jnp.pad(
        products.reshape(groups_here, block_rows * line_width), ((0, 0), (0, block_rows))
    )
    skewed = flat_rows.reshape(groups_here, block_rows, line_width + 1)[:, :, :tap_count]
    return jnp.sum(skewed, axis=1)[:, ::-1]


def featurize(padded, weights):
    short_reach = weights.shape[1] - 1
    row_count = padded.shape[1] - short_reach
    total = None
    for offset in range(weights.shape[1]):
        start = short_reach - offset
        term = weights[:, offset, :] * padded[:, start : start + row_count]
        total = term if total is None else total + term
    return total


def adjoint(padded, weights):
    short_reach = weights.shape[1] - 1
    row_count = padded.shape[1] - short_reach
    total = None
    for offset in range(weights.shape[1]):
        term = weights[:, offset, :] * padded[:, offset : offset + row_count]
        total = term if total is None else total + term
    return total


def short_sums(feature_grad, padded, short_taps):
    row_count = feature_grad.shape[1]
    short_reach = short_taps - 1
    terms = []
    for offset in range(short_taps):
        start = short_reach - offset
        terms.append(jnp.sum(feature_grad * padded[:, start : start + row_count], axis=(0, 1)))
    return jnp.stack(terms, axis=1)


def shards(projected, short_w, medium_h, out_w, grad_out):
    seq_local = projected.shape[0]
    row_count = projected.shape[1]
    chan_local = projected.shape[3]
    tap_count = medium_h.shape[1]
    reach = tap_count - 1
    short_taps = short_w.shape[1]
    short_reach = short_taps - 1
    group_local = medium_h.shape[0]
    group_size = chan_local // group_local
    block_rows = math.gcd(row_count, 128)
    front_rows = from_behind(projected[:, row_count - short_reach :], "ctx", 1)
    padded_input = jnp.concatenate([front_rows, projected], axis=1)
    features = featurize(padded_input.astype(jnp.float32), short_w)
    product = (features[:, :, 1] * features[:, :, 2]).astype(jnp.bfloat16)
    product_front = from_behind(product[:, row_count - reach :], "ctx", 1)
    product_pad = jnp.concatenate([product_front, product], axis=1)
    query = features[:, :, 0]
    keys = features[:, :, 1]
    values = features[:, :, 2]
    product_turned = jnp.swapaxes(
        product_pad.reshape(seq_local, row_count + reach, group_local, group_size), 2, 3
    )
    mixed = band_conv(product_turned, banded(medium_h[:, ::-1], block_rows), block_rows)
    gated = (query * mixed).astype(jnp.bfloat16)
    whole_gated = lax.all_gather(gated, "grp", axis=2, tiled=True)
    flat_gated = whole_gated.reshape(seq_local * row_count, whole_gated.shape[2])
    flat_cotangent = grad_out.reshape(seq_local * row_count, chan_local)
    projected_out = jnp.dot(
        flat_gated,
        lax.all_gather(out_w, "ctx", axis=0, tiled=True),
        preferred_element_type=jnp.float32,
    )
    block_out = projected_out.astype(jnp.bfloat16).reshape(seq_local, row_count, chan_local)
    input_part = lax.dot_general(
        flat_cotangent,
        lax.all_gather(out_w, "ctx", axis=0, tiled=True),
        (((1,), (1,)), ((), ())),
        preferred_element_type=jnp.float32,
    )
    summed = lax.psum_scatter(input_part, "grp", scatter_dimension=1, tiled=True)
    gated_grad = (
        lax.optimization_barrier(summed.astype(jnp.bfloat16))
        .astype(jnp.float32)
        .reshape(seq_local, row_count, chan_local)
    )
    query_grad = gated_grad * mixed
    mix_grad = (gated_grad * query).astype(jnp.bfloat16)
    mix_back = from_behind(mix_grad[:, :reach], "ctx", -1)
    mix_turned = jnp.swapaxes(
        jnp.concatenate([mix_grad, mix_back], axis=1).reshape(
            seq_local, row_count + reach, group_local, group_size
        ),
        2,
        3,
    )
    product_grad = band_conv(mix_turned, banded(medium_h, block_rows), block_rows)
    grad_blocks = jnp.swapaxes(
        mix_grad.reshape(seq_local, row_count // block_rows, block_rows, group_local, group_size),
        3,
        4,
    )
    filter_part = lag_sums(grad_blocks, windows(product_turned, block_rows, reach), tap_count)
    feature_grad = jnp.stack(
        [query_grad, product_grad * values, product_grad * keys], axis=2
    ).astype(jnp.bfloat16)
    grad_back = from_behind(feature_grad[:, :short_reach], "ctx", -1)
    grad_pad = jnp.concatenate([feature_grad, grad_back], axis=1).astype(jnp.float32)
    grad_projected = adjoint(grad_pad, short_w).astype(jnp.bfloat16)
    short_part = short_sums(
        feature_grad.astype(jnp.float32), padded_input.astype(jnp.float32), short_taps
    )
    filter_total, short_total = lax.psum((filter_part, short_part), ("dp", "ctx"))
    seq_total = seq_local * lax.axis_size("dp")
    length_total = row_count * lax.axis_size("ctx")
    filter_grad = filter_total / math.sqrt(seq_total * length_total * group_size)
    short_grad = short_total / math.sqrt(seq_total * length_total)
    return (block_out, grad_projected, filter_grad, short_grad)


def solution(mesh):
    in_specs = (
        P("dp", "ctx", None, "grp"),
        P(None, None, "grp"),
        P("grp", None),
        P("ctx", "grp"),
        P("dp", "ctx", "grp"),
    )
    out_specs = (
        P("dp", "ctx", "grp"),
        P("dp", "ctx", None, "grp"),
        P("grp", None),
        P(None, None, "grp"),
    )
    return jax.shard_map(shards, mesh=mesh, in_specs=in_specs, out_specs=out_specs, check_vma=False)
```

profile of v0, /device:TPU:1, one launch (start us, length us, event | category | flops | bytes accessed | tf_op | source)
XLA Modules:
  0.0 600.7 jit_solution(14814459723128327061)
XLA Ops:
  8.0 103.6 %all-gather.5.cloned.1.call-done = bf16[4096,1024]{1,0:T(8,128)(2,1)} async-done(((bf16[128,1024]{1,0:T(8,128)(2,1)}), bf16[4096,1024]{1,0:T(8,128)(2,1)}) %all-gather.5.cloned.1.call-update) | async-done | bytes 8388624 | tf_op jit(solution)/shard_map/all_gather | solution.py:127
  111.5 10.1 %fusion.31 = f32[512,4096]{1,0:T(8,128)} fusion(bf16[512,1024]{1,0:T(8,128)(2,1)S(1)} %bitcast.91, bf16[4096,1024]{1,0:T(8,128)(2,1)} %all-gather.5.cloned.1.call-done), kind=kOutput, calls=%fused_computation.57 | convolution fusion | flops 4294967296 | bytes 17825792 | tf_op jit(solution)/shard_map/dot_general | solution.py:131
  122.7 1.7 collective-permute-start
  124.5 4.6 copy.57
  130.0 4.6 maximum_convert_fusion
  134.6 3.6 copy-done.2
  138.3 5.9 multiply_add_fusion
  144.2 58.5 %reduce-scatter.2.cloned.1.call-done = f32[512,1024]{1,0:T(8,128)} async-done(((f32[512,4096]{1,0:T(8,128)}), f32[512,1024]{1,0:T(8,128)}) %reduce-scatter.2.cloned.1.call-update) | async-done | bytes 2097168 | tf_op jit(solution)/shard_map/reduce_scatter | solution.py:137
  202.6 1.7 convert_element_type.49
  204.6 1.8 copy.66
  206.4 2.4 fusion.14
  209.8 1.5 collective-permute-start.2
  211.6 2.6 copy.97
  214.2 2.3 slice.126
  216.5 15.8 %reshape.121 = bf16[64,128,255,1,1]{2,1,0,3,4:T(8,128)(2,1)} reshape(bf16[64,32640]{1,0:T(8,128)(2,1)} %slice.126) | data formatting | bytes 8355840 | tf_op jit(solution)/shard_map/reshape | solution.py:37
  232.3 1.6 pad_maximum_fusion.2
  233.9 1.5 fusion.29
  235.4 2.2 reshape.126
  237.5 2.5 copy.70
  240.1 2.1 reshape.127
  242.2 1.5 copy.95
  243.7 4.1 fusion.20
  247.8 2.4 copy.71
  250.3 3.9 reshape.116
  254.1 5.9 multiply_convert_fusion.1
  260.1 1.0 copy-done.7
  261.1 1.0 slice.119
  262.1 4.8 collective-permute-start.1
  267.3 2.6 copy.96
  269.9 2.3 slice.122
  272.2 16.0 %reshape.120 = bf16[64,128,255,1,1]{2,1,0,3,4:T(8,128)(2,1)} reshape(bf16[64,32640]{1,0:T(8,128)(2,1)} %slice.122) | data formatting | bytes 8355840 | tf_op jit(solution)/shard_map/reshape | solution.py:37
  288.2 1.6 copy.74
  289.8 1.9 copy.65
  291.7 2.6 reshape.117
  294.2 3.3 squeeze.10
  297.5 3.9 fusion.26
  301.4 1.8 pad_maximum_fusion.1
  303.2 1.2 pad_slice_fusion.1
  304.9 1.3 reshape.124
  306.8 1.3 copy-done.5
  308.1 3.7 fusion.17
  311.8 1.1 copy.62
  312.9 2.7 reshape.109
  315.6 3.0 reshape.104
  318.7 6.2 %convolution_bitcast_fusion = f32[64,128,255]{2,1,0:T(8,128)} fusion(bf16[2,2,255,16,64]{2,3,1,0,4:T(8,128)(2,1)} %copy-done.5, bf16[2,2,128,16,64]{2,1,0,3,4:T(2,128)(2,1)S(1)} %copy-done.9), kind=kOutput, calls=%fused_computation.20 | convolution fusion | flops 267386880 | bytes 11493376 | tf_op jit(solution)/shard_map/sbtcg,sbjcg->gtj/dot_general | solution.py:53
  324.9 9.2 %reshape.118 = f32[64,32640]{1,0:T(8,128)} reshape(f32[64,128,255]{2,1,0:T(8,128)} %convolution_bitcast_fusion) | data formatting | bytes 16711680 | tf_op jit(solution)/shard_map/reshape | solution.py:60
  334.1 4.0 pad.16
  338.2 2.5 copy.98
  341.9 2.4 multiply_convert_fusion.2
  344.4 10.9 %fusion = (f32[3,1024]{1,0:T(4,128)S(1)}, f32[3,1024]{1,0:T(4,128)S(1)}, f32[3,1024]{1,0:T(4,128)S(1)}) fusion(f32[2,258,3,1024]{1,3,0,2:T(8,128)} %copy-done.2, bf16[2,256,1,1024]{1,3,0,2:T(8,128)(2,1)S(1)} %copy-done.4, bf16[2,256,1,1024]{1,3,0,2:T(8,128)(2,1)S(1)} %copy-done.3, bf16[2,256,1,1024]{1,3,0,2:T(8,128)(2,1)S(1)} %multiply_convert_fusion.2), kind=kLoop, calls=%fused_computation.3 | loop fusion | flops 14146560 | bytes 22056960 | tf_op jit(solution)/shard_map/reduce_sum | solution.py:93
  356.0 3.4 fusion.13
  359.7 1.4 slice.127
  361.2 1.7 copy.72
  362.9 1.3 collective-permute-start.3
  364.2 3.3 collective-permute-done.3
  367.5 1.7 copy.73
  369.2 2.6 maximum_convert_fusion.1
  371.8 5.8 fusion.4
  377.6 4.6 copy.78
  382.2 145.3 %all-reduce.8.cloned.1.call-done = (f32[64,128]{1,0:T(8,128)}, f32[3,3,1024]{2,0,1:T(4,128)}) async-done(((f32[64,128]{1,0:T(8,128)}, f32[3,3,1024]{2,0,1:T(4,128)}), (f32[64,128]{1,0:T(8,128)}, f32[3,3,1024]{2,0,1:T(4,128)})) %all-reduce.8.cloned.1.call-update) | async-done | bytes 69648 | tf_op jit(solution)/shard_map/psum | solution.py:169
  529.1 1.4 broadcast_multiply_fusion.1
  530.4 46.8 %all-gather.3.cloned.1.call-done = bf16[2,256,4096]{1,2,0:T(8,128)(2,1)} async-done(((bf16[2,256,1024]{1,2,0:T(8,128)(2,1)}), bf16[2,256,4096]{1,2,0:T(8,128)(2,1)}) %all-gather.3.cloned.1.call-update) | async-done | bytes 4194320 | tf_op jit(solution)/shard_map/all_gather | solution.py:122
  577.3 6.5 %copy.63 = bf16[2,256,4096]{2,1,0:T(8,128)(2,1)} copy(bf16[2,256,4096]{1,2,0:T(8,128)(2,1)} %all-gather.3.cloned.1.call-done) | data formatting | bytes 8388608 | tf_op jit(solution)/shard_map/all_gather | solution.py:122
  583.8 10.2 %convolution_convert_fusion = bf16[512,1024]{1,0:T(8,128)(2,1)} fusion(bf16[512,4096]{1,0:T(8,128)(2,1)} %bitcast.102, bf16[4096,1024]{1,0:T(8,128)(2,1)} %all-gather.5.cloned.1.call-done), kind=kOutput, calls=%fused_computation.42 | convolution fusion | flops 4295491584 | bytes 13631488 | tf_op jit(solution)/shard_map/dot_general | solution.py:125
  (53 shorter events, 9.2 us)
Async XLA Ops:
  7.2 104.4 %copy-start = (bf16[2,256,1024]{2,1,0:T(8,128)(2,1)S(1)}, bf16[2,256,1024]{2,1,0:T(8,128)(2,1)}, u32[]{:S(2)}) copy-start(bf16[2,256,1024]{2,1,0:T(8,128)(2,1)} %param.9) | copy-start | bytes 3145732
  7.2 104.3 %all-gather.5.cloned.1.call-start = ((), (), s32[]{:S(2)}) async-start(), calls=%async_computation.2 | async-start | bytes 8650752 | tf_op jit(solution)/shard_map/all_gather | solution.py:127
  7.9 194.7 %reduce-scatter.2.cloned.1.call-start = ((), (), s32[]{:S(2)}) async-start(), calls=%async_computation.3 | async-start | bytes 10485760 | tf_op jit(solution)/shard_map/reduce_scatter | solution.py:137
  121.7 2.8 copy-start.11
  121.7 405.9 %all-reduce.8.cloned.1.call-start = ((), (), s32[]{:S(2)}) async-start(), calls=%async_computation.4 | async-start | bytes 163840 | tf_op jit(solution)/shard_map/psum | solution.py:169
  122.7 6.5 %collective-permute-start = (bf16[2,2,3,1024]{3,1,2,0:T(2,128)(2,1)S(1)}, bf16[2,2,3,1024]{3,1,2,0:T(2,128)(2,1)S(1)}, u32[]{:S(2)}, u32[]{:S(2)}) collective-permute-start(bf16[2,2,3,1024]{3,1,2,0:T(2,128)(2,1)S(1)} %slice.89), channel_id=1, source_target_pairs={{0,4},{4,8},{8,12},{12,16},{16,20},{20,24},{24,28},{28,32},{32,36}... | collective-permute-start | bytes 73736 | tf_op jit(solution)/shard_map/ppermute | solution.py:11
  134.6 3.7 copy-start.2
  206.4 4.8 copy-start.10
  208.9 2.4 copy-start.6
  209.8 22.5 %collective-permute-start.2 = (bf16[2,127,1024]{1,2,0:T(8,128)(2,1)}, bf16[2,127,1024]{1,2,0:T(8,128)(2,1)}, u32[]{:S(2)}, u32[]{:S(2)}) collective-permute-start(bf16[2,127,1024]{1,2,0:T(8,128)(2,1)} %slice.123), channel_id=1, source_target_pairs={{4,0},{8,4},{12,8},{16,12},{20,16},{24,20},{28,24},{32,28},{36,32}... | collective-permute-start | bytes 1560584 | tf_op jit(solution)/shard_map/ppermute | solution.py:11
  260.1 1.0 copy-start.7
  262.1 39.3 %collective-permute-start.1 = (bf16[2,127,1024]{1,2,0:T(8,128)(2,1)}, bf16[2,127,1024]{1,2,0:T(8,128)(2,1)}, u32[]{:S(2)}, u32[]{:S(2)}) collective-permute-start(bf16[2,127,1024]{1,2,0:T(8,128)(2,1)} %slice.119), channel_id=1, source_target_pairs={{0,4},{4,8},{8,12},{12,16},{16,20},{20,24},{24,28},{28,32},{32,36}... | collective-permute-start | bytes 1560584 | tf_op jit(solution)/shard_map/ppermute | solution.py:11
  297.5 3.9 copy-start.8
  306.7 1.3 copy-start.5
  315.6 3.0 copy-start.9
  341.2 3.2 copy-start.3
  341.2 3.2 copy-start.4
  355.9 221.4 %all-gather.3.cloned.1.call-start = ((), (), s32[]{:S(2)}) async-start(), calls=%async_computation.1 | async-start | bytes 5242880 | tf_op jit(solution)/shard_map/all_gather | solution.py:122
  362.9 4.6 collective-permute-start.3
  583.8 10.2 %copy-start.1 = (bf16[2,256,1024]{2,1,0:T(8,128)(2,1)S(1)}, bf16[2,256,1024]{2,1,0:T(8,128)(2,1)}, u32[]{:S(2)}) copy-start(bf16[2,256,1024]{2,1,0:T(8,128)(2,1)} %param.9) | copy-start | bytes 3145732
Sparse Core Ops, SparseCore 0:
  10.6 100.9 all-gather.4
  121.8 80.7 reduce-scatter.1
  356.0 171.5 all-reduce.7
  529.8 47.3 all-gather.2
where the time goes:
time: 607 us; the launch traced here: 601 us
  waiting for transfers between devices  358 us (59%)
  local copies, waits for them, and re-layouts  127 us (21%)
  other arithmetic  56.9 us (9%)
  matrix products  34.4 us (6%)
  between operations  14.3 us (2%)
  starting transfers between devices  9.42 us (2%)
    psum x1, waiting for transfers between devices, shards(): lax.psum((filter_part, short_part), ('dp', 'ctx'))  145 us
    all_gather x1, waiting for transfers between devices, shards(): lax.all_gather(out_w, 'ctx', axis=0, tiled=True)  104 us
    reduce_scatter x1, waiting for transfers between devices, shards(): lax.psum_scatter(input_part, 'grp', scatter_dimension=1, tiled=True)  58.5 us
    all_gather x1, waiting for transfers between devices, shards(): whole_gated = lax.all_gather(gated, 'grp', axis=2, tiled=True)  46.8 us
    reshape x2, local copies, waits for them, and re-layouts, banded(): tiled[:, :block_rows * (line_width - 1)]  31.8 us
    unnamed x34, local copies, waits for them, and re-layouts  25.5 us
  transfers between devices with their start and end apart: 8, of which 5 were waited for; matrix products, arithmetic and copies ran while one was open for 16% of the time, Pallas kernels for 0%

commit v1 on v0

--- a/solution.py
+++ b/solution.py
@@ -3,6 +3,11 @@
 import jax.numpy as jnp
 from jax import lax
 from jax.sharding import PartitionSpec as P
+
+
+def by_each_axis(value, first, second_2):
+    inner = lax.psum(value, first)
+    return lax.psum(inner, second_2)
 
 
 def from_behind(block, axis, distance):
@@ -166,7 +171,7 @@
     short_part = short_sums(
         feature_grad.astype(jnp.float32), padded_input.astype(jnp.float32), short_taps
     )
-    filter_total, short_total = lax.psum((filter_part, short_part), ("dp", "ctx"))
+    filter_total, short_total = by_each_axis((filter_part, short_part), "dp", "ctx")
     seq_total = seq_local * lax.axis_size("dp")
     length_total = row_count * lax.axis_size("ctx")
     filter_grad = filter_total / math.sqrt(seq_total * length_total * group_size)

time: 607 us -> 610 us (level)
    psum x1 -> x2, waiting for transfers between devices: 145 us -> 142 us  [the longest x1 116 us: by_each_axis(): return lax.psum(inner, second_2)]
    unnamed x34 -> x38, local copies, waits for them, and re-layouts: 25.5 us -> 25.6 us
  transfers between devices with their start and end apart: 8 -> 9, of which waited for: 5 -> 6; matrix products, arithmetic and copies ran while one was open for 16% -> 17% of each run, Pallas kernels for 0% -> 0%
where the time goes in v1:
time: 610 us; the launch traced here: 603 us
  waiting for transfers between devices  360 us (59%)
  local copies, waits for them, and re-layouts  128 us (21%)
  other arithmetic  57.5 us (9%)
  matrix products  34.4 us (6%)
  between operations  14.3 us (2%)
  starting transfers between devices  9.46 us (2%)
    psum x1, waiting for transfers between devices, by_each_axis(): return lax.psum(inner, second_2)  116 us
    all_gather x1, waiting for transfers between devices, shards(): lax.all_gather(out_w, 'ctx', axis=0, tiled=True)  104 us
    reduce_scatter x1, waiting for transfers between devices, shards(): lax.psum_scatter(input_part, 'grp', scatter_dimension=1, tiled=True)  58.5 us
    all_gather x1, waiting for transfers between devices, shards(): whole_gated = lax.all_gather(gated, 'grp', axis=2, tiled=True)  51.6 us
    reshape x2, local copies, waits for them, and re-layouts, banded(): tiled[:, :block_rows * (line_width - 1)]  31.9 us
    psum x1, waiting for transfers between devices, by_each_axis(): inner = lax.psum(value, first)  26.4 us
    unnamed x38, local copies, waits for them, and re-layouts  25.6 us
  transfers between devices with their start and end apart: 9, of which 6 were waited for; matrix products, arithmetic and copies ran while one was open for 17% of the time, Pallas kernels for 0%

profile of v1, /device:TPU:1, one launch (start us, length us, event | category | flops | bytes accessed | tf_op | source)
XLA Modules:
  0.0 603.0 jit_solution(9203216123000702300)
XLA Ops:
  8.0 103.6 %all-gather.5.cloned.1.call-done = bf16[4096,1024]{1,0:T(8,128)(2,1)} async-done(((bf16[128,1024]{1,0:T(8,128)(2,1)}), bf16[4096,1024]{1,0:T(8,128)(2,1)}) %all-gather.5.cloned.1.call-update) | async-done | bytes 8388624 | tf_op jit(solution)/shard_map/all_gather | solution.py:132
  111.5 10.2 %fusion.31 = f32[512,4096]{1,0:T(8,128)} fusion(bf16[512,1024]{1,0:T(8,128)(2,1)S(1)} %bitcast.91, bf16[4096,1024]{1,0:T(8,128)(2,1)} %all-gather.5.cloned.1.call-done), kind=kOutput, calls=%fused_computation.57 | convolution fusion | flops 4294967296 | bytes 17825792 | tf_op jit(solution)/shard_map/dot_general | solution.py:136
  122.7 1.7 collective-permute-start
  124.5 4.6 copy.57
  130.1 4.6 maximum_convert_fusion
  134.6 3.7 copy-done.2
  138.3 5.9 multiply_add_fusion
  144.2 58.5 %reduce-scatter.2.cloned.1.call-done = f32[512,1024]{1,0:T(8,128)} async-done(((f32[512,4096]{1,0:T(8,128)}), f32[512,1024]{1,0:T(8,128)}) %reduce-scatter.2.cloned.1.call-update) | async-done | bytes 2097168 | tf_op jit(solution)/shard_map/reduce_scatter | solution.py:142
  202.7 1.7 convert_element_type.49
  204.7 1.8 copy.66
  206.5 2.4 fusion.14
  209.8 1.5 collective-permute-start.2
  211.6 2.6 copy.97
  214.2 2.3 slice.126
  216.5 15.8 %reshape.121 = bf16[64,128,255,1,1]{2,1,0,3,4:T(8,128)(2,1)} reshape(bf16[64,32640]{1,0:T(8,128)(2,1)} %slice.126) | data formatting | bytes 8355840 | tf_op jit(solution)/shard_map/reshape | solution.py:42
  232.3 1.6 pad_maximum_fusion.2
  233.9 1.5 fusion.29
  235.4 2.1 reshape.126
  237.6 2.5 copy.70
  240.1 2.1 reshape.127
  242.2 1.5 copy.95
  243.7 4.1 fusion.20
  247.8 2.4 copy.71
  250.3 3.9 reshape.116
  254.2 5.9 multiply_convert_fusion.1
  261.1 1.0 slice.119
  262.1 4.8 collective-permute-start.1
  267.3 2.6 copy.96
  269.9 2.3 slice.122
  272.2 16.0 %reshape.120 = bf16[64,128,255,1,1]{2,1,0,3,4:T(8,128)(2,1)} reshape(bf16[64,32640]{1,0:T(8,128)(2,1)} %slice.122) | data formatting | bytes 8355840 | tf_op jit(solution)/shard_map/reshape | solution.py:42
  288.2 1.6 copy.74
  289.8 1.8 copy.65
  291.7 2.6 reshape.117
  294.2 3.3 squeeze.10
  297.5 3.9 fusion.26
  301.4 1.8 pad_maximum_fusion.1
  303.2 1.2 pad_slice_fusion.1
  304.9 1.3 reshape.124
  306.8 1.3 copy-done.7
  308.0 3.7 fusion.17
  311.8 1.1 copy.62
  312.9 2.7 reshape.109
  315.6 6.2 %convolution_bitcast_fusion = f32[64,128,255]{2,1,0:T(8,128)} fusion(bf16[2,2,255,16,64]{2,3,1,0,4:T(8,128)(2,1)} %copy-done.7, bf16[2,2,128,16,64]{2,1,0,3,4:T(2,128)(2,1)S(1)} %copy-done.11), kind=kOutput, calls=%fused_computation.20 | convolution fusion | flops 267386880 | bytes 11493376 | tf_op jit(solution)/shard_map/sbtcg,sbjcg->gtj/dot_general | solution.py:58
  321.8 9.6 %reshape.118 = f32[64,32640]{1,0:T(8,128)} reshape(f32[64,128,255]{2,1,0:T(8,128)} %convolution_bitcast_fusion) | data formatting | bytes 16711680 | tf_op jit(solution)/shard_map/reshape | solution.py:65
  331.5 4.0 pad.16
  335.5 2.5 copy.98
  339.2 2.6 multiply_convert_fusion.2
  342.0 11.2 %fusion = (f32[3,1024]{1,0:T(4,128)S(1)}, f32[3,1024]{1,0:T(4,128)S(1)}, f32[3,1024]{1,0:T(4,128)S(1)}) fusion(f32[2,258,3,1024]{1,3,0,2:T(8,128)} %copy-done.2, bf16[2,256,1,1024]{1,3,0,2:T(8,128)(2,1)S(1)} %copy-done.5, bf16[2,256,1,1024]{1,3,0,2:T(8,128)(2,1)S(1)} %copy-done.3, bf16[2,256,1,1024]{1,3,0,2:T(8,128)(2,1)S(1)} %multiply_convert_fusion.2), kind=kLoop, calls=%fused_computation.3 | loop fusion | flops 14146560 | bytes 22056960 | tf_op jit(solution)/shard_map/reduce_sum | solution.py:98
  353.9 2.7 reshape.104
  356.6 26.4 %all-reduce.12.cloned.1.call-done = (f32[64,128]{1,0:T(8,128)}, f32[3,3,1024]{2,0,1:T(4,128)}) async-done(((f32[64,128]{1,0:T(8,128)}, f32[3,3,1024]{2,0,1:T(4,128)}), (f32[64,128]{1,0:T(8,128)}, f32[3,3,1024]{2,0,1:T(4,128)})) %all-reduce.12.cloned.1.call-update) | async-done | bytes 69648 | tf_op jit(solution)/shard_map/psum | solution.py:9
  383.1 3.6 fusion.13
  387.1 1.4 slice.127
  388.5 1.7 copy.72
  390.2 1.3 collective-permute-start.3
  391.5 3.3 collective-permute-done.3
  394.8 1.7 copy.73
  396.6 2.6 maximum_convert_fusion.1
  399.2 5.8 fusion.4
  405.0 4.6 copy.78
  409.6 115.5 %all-reduce.10.cloned.1.call-done = (f32[64,128]{1,0:T(8,128)}, f32[3,3,1024]{2,0,1:T(4,128)}) async-done(((f32[64,128]{1,0:T(8,128)}, f32[3,3,1024]{2,0,1:T(4,128)}), (f32[64,128]{1,0:T(8,128)}, f32[3,3,1024]{2,0,1:T(4,128)})) %all-reduce.10.cloned.1.call-update) | async-done | bytes 69648 | tf_op jit(solution)/shard_map/psum | solution.py:10
  526.6 1.4 broadcast_multiply_fusion.1
  528.0 51.6 %all-gather.3.cloned.1.call-done = bf16[2,256,4096]{1,2,0:T(8,128)(2,1)} async-done(((bf16[2,256,1024]{1,2,0:T(8,128)(2,1)}), bf16[2,256,4096]{1,2,0:T(8,128)(2,1)}) %all-gather.3.cloned.1.call-update) | async-done | bytes 4194320 | tf_op jit(solution)/shard_map/all_gather | solution.py:127
  579.6 6.5 %copy.63 = bf16[2,256,4096]{2,1,0:T(8,128)(2,1)} copy(bf16[2,256,4096]{1,2,0:T(8,128)(2,1)} %all-gather.3.cloned.1.call-done) | data formatting | bytes 8388608 | tf_op jit(solution)/shard_map/all_gather | solution.py:127
  586.1 10.2 %convolution_convert_fusion = bf16[512,1024]{1,0:T(8,128)(2,1)} fusion(bf16[512,4096]{1,0:T(8,128)(2,1)} %bitcast.102, bf16[4096,1024]{1,0:T(8,128)(2,1)} %all-gather.5.cloned.1.call-done), kind=kOutput, calls=%fused_computation.42 | convolution fusion | flops 4295491584 | bytes 13631488 | tf_op jit(solution)/shard_map/dot_general | solution.py:130
  (60 shorter events, 10.5 us)
Async XLA Ops:
  7.2 104.4 %copy-start = (bf16[2,256,1024]{2,1,0:T(8,128)(2,1)S(1)}, bf16[2,256,1024]{2,1,0:T(8,128)(2,1)}, u32[]{:S(2)}) copy-start(bf16[2,256,1024]{2,1,0:T(8,128)(2,1)} %param.9) | copy-start | bytes 3145732
  7.2 104.3 %all-gather.5.cloned.1.call-start = ((), (), s32[]{:S(2)}) async-start(), calls=%async_computation.2 | async-start | bytes 8650752 | tf_op jit(solution)/shard_map/all_gather | solution.py:132
  7.9 194.7 %reduce-scatter.2.cloned.1.call-start = ((), (), s32[]{:S(2)}) async-start(), calls=%async_computation.3 | async-start | bytes 10485760 | tf_op jit(solution)/shard_map/reduce_scatter | solution.py:142
  121.7 2.8 copy-start.13
  121.7 261.3 %all-reduce.12.cloned.1.call-start = ((), (), s32[]{:S(2)}) async-start(), calls=%async_computation.5 | async-start | bytes 163840 | tf_op jit(solution)/shard_map/psum | solution.py:9
  122.7 6.5 %collective-permute-start = (bf16[2,2,3,1024]{3,1,2,0:T(2,128)(2,1)S(1)}, bf16[2,2,3,1024]{3,1,2,0:T(2,128)(2,1)S(1)}, u32[]{:S(2)}, u32[]{:S(2)}) collective-permute-start(bf16[2,2,3,1024]{3,1,2,0:T(2,128)(2,1)S(1)} %slice.89), channel_id=1, source_target_pairs={{0,4},{4,8},{8,12},{12,16},{16,20},{20,24},{24,28},{28,32},{32,36}... | collective-permute-start | bytes 73736 | tf_op jit(solution)/shard_map/ppermute | solution.py:16
  134.6 3.7 copy-start.2
  206.5 4.8 copy-start.12
  208.9 2.4 copy-start.8
  209.8 22.5 %collective-permute-start.2 = (bf16[2,127,1024]{1,2,0:T(8,128)(2,1)}, bf16[2,127,1024]{1,2,0:T(8,128)(2,1)}, u32[]{:S(2)}, u32[]{:S(2)}) collective-permute-start(bf16[2,127,1024]{1,2,0:T(8,128)(2,1)} %slice.123), channel_id=1, source_target_pairs={{4,0},{8,4},{12,8},{16,12},{20,16},{24,20},{28,24},{32,28},{36,32}... | collective-permute-start | bytes 1560584 | tf_op jit(solution)/shard_map/ppermute | solution.py:16
  260.1 1.0 copy-start.9
  262.1 39.3 %collective-permute-start.1 = (bf16[2,127,1024]{1,2,0:T(8,128)(2,1)}, bf16[2,127,1024]{1,2,0:T(8,128)(2,1)}, u32[]{:S(2)}, u32[]{:S(2)}) collective-permute-start(bf16[2,127,1024]{1,2,0:T(8,128)(2,1)} %slice.119), channel_id=1, source_target_pairs={{0,4},{4,8},{8,12},{12,16},{16,20},{20,24},{24,28},{28,32},{32,36}... | collective-permute-start | bytes 1560584 | tf_op jit(solution)/shard_map/ppermute | solution.py:16
  297.5 3.9 copy-start.10
  306.8 1.3 copy-start.7
  312.9 2.7 copy-start.11
  339.2 2.6 copy-start.3
  339.2 2.8 copy-start.5
  353.9 171.3 %all-reduce.10.cloned.1.call-start = ((), (), s32[]{:S(2)}) async-start(), calls=%async_computation.4 | async-start | bytes 163840 | tf_op jit(solution)/shard_map/psum | solution.py:10
  383.0 3.7 copy-start.4
  383.0 3.7 copy-start.6
  383.0 196.6 %all-gather.3.cloned.1.call-start = ((), (), s32[]{:S(2)}) async-start(), calls=%async_computation.1 | async-start | bytes 5242880 | tf_op jit(solution)/shard_map/all_gather | solution.py:127
  390.2 4.6 collective-permute-start.3
  586.1 10.2 %copy-start.1 = (bf16[2,256,1024]{2,1,0:T(8,128)(2,1)S(1)}, bf16[2,256,1024]{2,1,0:T(8,128)(2,1)}, u32[]{:S(2)}) copy-start(bf16[2,256,1024]{2,1,0:T(8,128)(2,1)} %param.9) | copy-start | bytes 3145732
Sparse Core Ops, SparseCore 0:
  10.6 100.9 all-gather.4
  121.8 80.7 reduce-scatter.1
  354.0 28.9 all-reduce.11
  386.3 138.7 all-reduce.9
  526.8 52.7 all-gather.2
